TPU v7x, 512 devices: a whole 4x4x16 slice. The times are simulated.
512 devices in a mesh: dp: 16 (over z), row: 8 (over y, core), col: 4 (over x).
Axes of the slice: x: 4, y: 4, z: 16, core: 2. Of those that a mesh axis runs over, the one named last changes fastest.
Arguments:
- grad_blocks: bfloat16 [16, 4096, 1024], P('dp', 'row', 'col'), may hold values from -300 to 300
- ln_grads: bfloat16 [16, 4, 1024], P('dp', None, 'col'), may hold values from -240 to 240, as said below
- master: float32 [4096, 1024], P(('row', 'col')), may hold values from -6 to 6
- first_moment: float32 [4096, 1024], P(('row', 'col')), may hold values from -6 to 6
- second_moment: float32 [4096, 1024], P(('row', 'col')), may hold values from 0.3 to 3
- average: float32 [4096, 1024], P('row', 'col'), may hold values from -6 to 6
- ln_master: float32 [4, 1024], P(None, 'col'), may hold values from -6 to 6
- ln_first: float32 [4, 1024], P(None, 'col'), may hold values from -6 to 6
- ln_second: float32 [4, 1024], P(None, 'col'), may hold values from 0.3 to 3
- ln_average: float32 [4, 1024], P(None, 'col'), may hold values from -6 to 6
Outputs:
- average_new: float32 [4096, 1024], P('row', 'col')
- master_new: float32 [4096, 1024], P(('row', 'col'))
- first_new: float32 [4096, 1024], P(('row', 'col'))
- second_new: float32 [4096, 1024], P(('row', 'col'))
- ln_master_new: float32 [4, 1024], P(None, 'col')
- ln_first_new: float32 [4, 1024], P(None, 'col')
- ln_second_new: float32 [4, 1024], P(None, 'col')
- ln_average_new: float32 [4, 1024], P(None, 'col')
Inputs may be any that keep to these rules, and one draw needn't show every extreme that they name: `ln_grads`: partial gradients of each data-parallel group.
All inputs are finite; a program needn't handle non-finite values.
Results may differ from a plain program's by a relative error of at most 0.0003.
Values may be sent and summed in bfloat16 or wider, within the bound.
A program may use at most 64 MiB of HBM per device.

v0:
```python
import math
import jax
import jax.numpy as jnp
from jax import lax
from jax.sharding import PartitionSpec as P

D = 1024
FF = 4096
STEP = 20
beta_one = 0.9
beta_two = 0.95
learn_rate = 0.02
decay_rate = 0.1
epsilon = 1e-08
clip_rms = 1.0
ema_keep = 0.9


def adam_step(gradient, clip_scale, first, second, master, decay_weight):
    clipped = clip_scale * gradient
    first_new = beta_one * first + (1.0 - beta_one) * clipped
    second_new = beta_two * second + (1.0 - beta_two) * clipped * clipped
    direction = (
        first_new
        / (1.0 - beta_one**STEP)
        / (jnp.sqrt(second_new / (1.0 - beta_two**STEP)) + epsilon)
    )
    master_new = master - learn_rate * (direction + decay_weight * master)
    return (master_new, first_new, second_new)


def clip_factor(norm_total):
    return jnp.minimum(1.0, clip_rms * math.sqrt(FF * D + 4 * D) / jnp.sqrt(norm_total))


def squares(gradient, ln_gradient, row_count):
    return jnp.sum(gradient * gradient) + jnp.sum(ln_gradient * ln_gradient) / row_count


def shards(
    grad_blocks,
    ln_grads,
    master,
    first_moment,
    second_moment,
    average,
    ln_master,
    ln_first,
    ln_second,
    ln_average,
):
    row_count = float(lax.axis_size("row"))
    summed, ln_gradient = lax.psum(
        (grad_blocks[0].astype(jnp.float32), ln_grads[0].astype(jnp.float32)), "dp"
    )
    gradient = lax.all_to_all(summed, "col", split_axis=0, concat_axis=1, tiled=True)
    norm_total = lax.psum(squares(gradient, ln_gradient, row_count), ("row", "col"))
    clip_scale = clip_factor(norm_total)
    master_new, first_new, second_new = adam_step(
        gradient, clip_scale, first_moment, second_moment, master, decay_rate
    )
    ln_master_new, ln_first_new, ln_second_new = adam_step(
        ln_gradient, clip_scale, ln_first, ln_second, ln_master, 0.0
    )
    ln_average_new = ema_keep * ln_average + (1.0 - ema_keep) * ln_master_new
    block_master = lax.all_to_all(master_new, "col", split_axis=1, concat_axis=0, tiled=True)
    average_new = ema_keep * average + (1.0 - ema_keep) * block_master
    return (
        average_new,
        master_new,
        first_new,
        second_new,
        ln_master_new,
        ln_first_new,
        ln_second_new,
        ln_average_new,
    )


def solution(mesh):
    placed = (
        P("dp", "row", "col"),
        P("dp", None, "col"),
        P(("row", "col"), None),
        P(("row", "col"), None),
        P(("row", "col"), None),
        P("row", "col"),
        P(None, "col"),
        P(None, "col"),
        P(None, "col"),
        P(None, "col"),
    )
    return jax.shard_map(
        shards,
        mesh=mesh,
        in_specs=placed,
        out_specs=(
            P("row", "col"),
            P(("row", "col"), None),
            P(("row", "col"), None),
            P(("row", "col"), None),
            P(None, "col"),
            P(None, "col"),
            P(None, "col"),
            P(None, "col"),
        ),
        check_vma=False,
    )
```

profile of v0, /device:TPU:2, one launch (start us, length us, event | category | flops | bytes accessed | tf_op | source)
XLA Modules:
  0.0 162.7 jit_solution(14626310819225786435)
XLA Ops:
  0.6 0.7 bitcast_convert_fusion
  1.3 69.7 %all-reduce.2 = (f32[4,128,256]{2,1,0:T(8,128)}, f32[4,256]{1,0:T(4,128)S(1)}) all-reduce(bf16[4,128,256]{2,1,0:T(8,128)(2,1)} %bitcast.20, f32[4,256]{1,0:T(4,128)S(1)} %bitcast_convert_fusion), channel_id=1, replica_groups=mesh['dp'=16,'row'=8,'col'=4] {'dp'}, use_global_device_ids=true, to_apply=%region_0.0 | all-reduce | flops 132096 | bytes 794624 | tf_op jit(solution)/shard_map/psum | solution.py:53
  71.0 0.0 copy-start.1
  71.0 5.0 %all-to-all-start = ((f32[4,128,256]{2,1,0:T(8,128)}), f32[4,128,256]{2,1,0:T(8,128)S(1)}, u32[]{:S(2)}, u32[]{:S(2)}) async-start(f32[4,128,256]{2,1,0:T(8,128)} %get-tuple-element.16), calls=%async_computation | async-start | bytes 1048576 | tf_op jit(solution)/shard_map/all_to_all | solution.py:56
  76.0 0.0 copy-done.1
  76.0 0.0 copy-start.2
  76.0 0.2 copy.24
  76.2 0.8 copy-done.2
  77.0 0.2 copy.20
  77.2 0.0 copy-start.3
  77.2 0.6 multiply_reduce_fusion.1
  78.5 4.1 %all-to-all-done = f32[4,128,256]{2,1,0:T(8,128)S(1)} async-done(((f32[4,128,256]{2,1,0:T(8,128)}), f32[4,128,256]{2,1,0:T(8,128)S(1)}, u32[]{:S(2)}, u32[]{:S(2)}) %all-to-all-start) | async-done | bytes 524320 | tf_op jit(solution)/shard_map/all_to_all | solution.py:56
  82.6 0.7 multiply_reduce_fusion
  84.0 0.0 copy-done.3
  84.0 0.2 copy.22
  84.2 64.9 %psum.23 = f32[]{:T(128)} all-reduce(f32[]{:T(128)S(6)} %add.45), channel_id=1, replica_groups=mesh['dp'=16,'row'=8,'col'=4] {'row','col'}, use_global_device_ids=true, to_apply=%region_4.0 | all-reduce | flops 1 | bytes 8 | tf_op jit(solution)/shard_map/psum | solution.py:57
  149.8 0.2 copy.21
  150.0 0.4 multiply_subtract_fusion
  150.4 1.0 copy.25
  151.4 3.7 %all-to-all-start.1 = ((f32[128,4,256]{2,0,1:T(8,128)}), f32[128,4,256]{2,0,1:T(8,128)S(1)}, u32[]{:S(2)}, u32[]{:S(2)}) async-start(f32[128,4,256]{2,0,1:T(8,128)} %copy.25), calls=%async_computation.1 | async-start | bytes 1048576 | tf_op jit(solution)/shard_map/all_to_all | solution.py:66
  155.2 1.0 copy.26
  156.2 1.0 copy.27
  157.2 0.0 copy-start.4
  157.2 0.0 copy-start.5
  157.2 0.0 copy-start.6
  157.2 0.0 copy-start.7
  157.2 1.0 copy.28
  158.2 0.0 copy-done.4
  158.2 0.0 copy-done.5
  158.2 0.0 copy-done.6
  158.2 0.0 copy-done.7
  158.2 0.6 multiply_add_fusion
  158.8 0.0 copy-start
  158.8 3.0 %all-to-all-done.1 = f32[128,4,256]{2,0,1:T(8,128)S(1)} async-done(((f32[128,4,256]{2,0,1:T(8,128)}), f32[128,4,256]{2,0,1:T(8,128)S(1)}, u32[]{:S(2)}, u32[]{:S(2)}) %all-to-all-start.1) | async-done | bytes 524320 | tf_op jit(solution)/shard_map/all_to_all | solution.py:66
  161.9 0.0 copy-done
  161.9 0.9 bitcast_add_fusion
  (2 shorter events, 0.1 us)
Async XLA Ops:
  71.0 5.0 %copy-start.1 = (f32[128,1024]{1,0:T(8,128)S(1)}, f32[128,1024]{1,0:T(8,128)}, u32[]{:S(2)}) copy-start(f32[128,1024]{1,0:T(8,128)} %param.12) | copy-start | bytes 1572868
  71.0 11.6 %all-to-all-start = ((f32[4,128,256]{2,1,0:T(8,128)}), f32[4,128,256]{2,1,0:T(8,128)S(1)}, u32[]{:S(2)}, u32[]{:S(2)}) async-start(f32[4,128,256]{2,1,0:T(8,128)} %get-tuple-element.16), calls=%async_computation | async-start | bytes 1048576 | tf_op jit(solution)/shard_map/all_to_all | solution.py:56
  76.0 1.0 copy-start.2
  77.2 6.8 %copy-start.3 = (f32[128,1024]{1,0:T(8,128)S(1)}, f32[128,1024]{1,0:T(8,128)}, u32[]{:S(2)}) copy-start(f32[128,1024]{1,0:T(8,128)} %param.14) | copy-start | bytes 1572868
  151.4 10.4 %all-to-all-start.1 = ((f32[128,4,256]{2,0,1:T(8,128)}), f32[128,4,256]{2,0,1:T(8,128)S(1)}, u32[]{:S(2)}, u32[]{:S(2)}) async-start(f32[128,4,256]{2,0,1:T(8,128)} %copy.25), calls=%async_computation.1 | async-start | bytes 1048576 | tf_op jit(solution)/shard_map/all_to_all | solution.py:66
  157.2 1.0 copy-start.4
  157.2 1.0 copy-start.5
  157.2 1.0 copy-start.6
  157.2 1.0 copy-start.7
  158.8 3.0 %copy-start = (f32[512,256]{1,0:T(8,128)S(1)}, f32[512,256]{1,0:T(8,128)}, u32[]{:S(2)}) copy-start(f32[512,256]{1,0:T(8,128)} %param.15) | copy-start | bytes 1572868
where the time goes:
time: 163 us
  blocking collectives  135 us (83%)
  starting transfers between devices  8.69 us (5%)
  waiting for transfers between devices  7.11 us (4%)
  local copies, waits for them, and re-layouts  5.61 us (3%)
  other arithmetic  4.02 us (2%)
  between operations  2.72 us (2%)
    psum x1, blocking collectives, shards(): lax.psum((grad_blocks[0].astype(jnp.float32), ln_grads[0].astype(jnp.floa...  69.7 us
    psum x1, blocking collectives, shards(): lax.psum(squares(gradient, ln_gradient, row_count), ('row', 'col'))  64.9 us
    all_to_all x1, starting transfers between devices, shards(): lax.all_to_all(summed, 'col', split_axis=0, concat_axis=1, tiled=True)  4.96 us
    unnamed x22, local copies, waits for them, and re-layouts  4.42 us
    all_to_all x1, waiting for transfers between devices, shards(): lax.all_to_all(summed, 'col', split_axis=0, concat_axis=1, tiled=True)  4.12 us
    all_to_all x1, starting transfers between devices, shards(): lax.all_to_all(master_new, 'col', split_axis=1, concat_axis=0, tiled=True)  3.73 us
  transfers between devices with their start and end apart: 2, of which 2 were waited for; matrix products, arithmetic and copies ran while one was open for 3% of the time, Pallas kernels for 0%

commit v1 on v0

--- a/solution.py
+++ b/solution.py
@@ -54,7 +54,7 @@
         (grad_blocks[0].astype(jnp.float32), ln_grads[0].astype(jnp.float32)), "dp"
     )
     gradient = lax.all_to_all(summed, "col", split_axis=0, concat_axis=1, tiled=True)
-    norm_total = lax.psum(squares(gradient, ln_gradient, row_count), ("row", "col"))
+    norm_total = lax.psum(lax.psum(squares(gradient, ln_gradient, row_count), "col"), "row")
     clip_scale = clip_factor(norm_total)
     master_new, first_new, second_new = adam_step(
         gradient, clip_scale, first_moment, second_moment, master, decay_rate

time: 163 us -> 125 us (0.77)
  the two profiles are of different devices: /device:TPU:2 before, /device:TPU:1 now
where the time goes in v1:
time: 125 us
  blocking collectives  94.6 us (76%)
  waiting for transfers between devices  10.9 us (9%)
  starting transfers between devices  7.62 us (6%)
  local copies, waits for them, and re-layouts  4.77 us (4%)
  other arithmetic  4.02 us (3%)
  between operations  2.73 us (2%)
    psum x1, blocking collectives, shards(): lax.psum((grad_blocks[0].astype(jnp.float32), ln_grads[0].astype(jnp.floa...  56.8 us
    psum x1, blocking collectives, shards(): lax.psum(lax.psum(squares(gradient, ln_gradient, row_count), 'col'), 'row')  30.4 us
    psum x1, blocking collectives, shards(): lax.psum(squares(gradient, ln_gradient, row_count), 'col')  7.39 us
    all_to_all x1, waiting for transfers between devices, shards(): lax.all_to_all(summed, 'col', split_axis=0, concat_axis=1, tiled=True)  5.47 us
    all_to_all x1, waiting for transfers between devices, shards(): lax.all_to_all(master_new, 'col', split_axis=1, concat_axis=0, tiled=True)  5.44 us
    all_to_all x1, starting transfers between devices, shards(): lax.all_to_all(summed, 'col', split_axis=0, concat_axis=1, tiled=True)  4.14 us
    unnamed x22, local copies, waits for them, and re-layouts  3.59 us
    all_to_all x1, starting transfers between devices, shards(): lax.all_to_all(master_new, 'col', split_axis=1, concat_axis=0, tiled=True)  3.47 us
  transfers between devices with their start and end apart: 2, of which 2 were waited for; matrix products, arithmetic and copies ran while one was open for 4% of the time, Pallas kernels for 0%

profile of v1, /device:TPU:1, one launch (start us, length us, event | category | flops | bytes accessed | tf_op | source)
XLA Modules:
  0.0 124.7 jit_solution(11046799451126062905)
XLA Ops:
  0.6 0.7 bitcast_convert_fusion
  1.3 56.8 %all-reduce.2 = (f32[4,128,256]{2,1,0:T(8,128)}, f32[4,256]{1,0:T(4,128)S(1)}) all-reduce(bf16[4,128,256]{2,1,0:T(8,128)(2,1)} %bitcast.20, f32[4,256]{1,0:T(4,128)S(1)} %bitcast_convert_fusion), channel_id=1, replica_groups=mesh['dp'=16,'row'=8,'col'=4] {'dp'}, use_global_device_ids=true, to_apply=%region_0.0 | all-reduce | flops 132096 | bytes 794624 | tf_op jit(solution)/shard_map/psum | solution.py:53
  58.1 0.0 copy-start.1
  58.1 4.1 %all-to-all-start = ((f32[4,128,256]{2,1,0:T(8,128)}), f32[4,128,256]{2,1,0:T(8,128)S(1)}, u32[]{:S(2)}, u32[]{:S(2)}) async-start(f32[4,128,256]{2,1,0:T(8,128)} %get-tuple-element.16), calls=%async_computation | async-start | bytes 1048576 | tf_op jit(solution)/shard_map/all_to_all | solution.py:56
  62.3 0.0 copy-done.1
  62.3 0.2 copy.24
  62.5 0.0 copy-start.2
  62.5 0.6 multiply_reduce_fusion.1
  63.8 5.5 %all-to-all-done = f32[4,128,256]{2,1,0:T(8,128)S(1)} async-done(((f32[4,128,256]{2,1,0:T(8,128)}), f32[4,128,256]{2,1,0:T(8,128)S(1)}, u32[]{:S(2)}, u32[]{:S(2)}) %all-to-all-start) | async-done | bytes 524320 | tf_op jit(solution)/shard_map/all_to_all | solution.py:56
  69.2 0.7 multiply_reduce_fusion
  70.6 0.0 copy-done.2
  70.6 0.0 copy-start.3
  70.6 0.2 copy.20
  70.8 7.4 %psum.30 = f32[]{:T(128)} all-reduce(f32[]{:T(128)S(6)} %add.47), channel_id=1, replica_groups=mesh['dp'=16,'row'=8,'col'=4] {'col'}, use_global_device_ids=true, to_apply=%region_4.0 | all-reduce | flops 1 | bytes 8 | tf_op jit(solution)/shard_map/psum | solution.py:57
  78.2 0.0 copy-done.3
  78.2 0.2 copy.22
  78.4 30.4 %psum.31 = f32[]{:T(128)} all-reduce(f32[]{:T(128)} %psum.30), channel_id=1, replica_groups=mesh['dp'=16,'row'=8,'col'=4] {'row'}, use_global_device_ids=true, to_apply=%region_5.0 | all-reduce | flops 1 | bytes 8 | tf_op jit(solution)/shard_map/psum | solution.py:57
  109.5 0.2 copy.21
  109.7 0.4 multiply_subtract_fusion
  110.2 1.0 copy.25
  111.2 3.5 %all-to-all-start.1 = ((f32[128,4,256]{2,0,1:T(8,128)}), f32[128,4,256]{2,0,1:T(8,128)S(1)}, u32[]{:S(2)}, u32[]{:S(2)}) async-start(f32[128,4,256]{2,0,1:T(8,128)} %copy.25), calls=%async_computation.1 | async-start | bytes 1048576 | tf_op jit(solution)/shard_map/all_to_all | solution.py:66
  114.6 1.0 copy.26
  115.6 1.0 copy.27
  116.6 0.0 copy-start.4
  116.6 0.0 copy-start.5
  116.6 0.0 copy-start.6
  116.6 0.0 copy-start.7
  116.6 1.0 copy.28
  117.6 0.0 copy-done.4
  117.6 0.0 copy-done.5
  117.6 0.0 copy-done.6
  117.6 0.0 copy-done.7
  117.7 0.6 multiply_add_fusion
  118.3 0.0 copy-start
  118.3 5.4 %all-to-all-done.1 = f32[128,4,256]{2,0,1:T(8,128)S(1)} async-done(((f32[128,4,256]{2,0,1:T(8,128)}), f32[128,4,256]{2,0,1:T(8,128)S(1)}, u32[]{:S(2)}, u32[]{:S(2)}) %all-to-all-start.1) | async-done | bytes 524320 | tf_op jit(solution)/shard_map/all_to_all | solution.py:66
  123.8 0.0 copy-done
  123.8 0.9 bitcast_add_fusion
  (2 shorter events, 0.1 us)
Async XLA Ops:
  58.1 4.1 %copy-start.1 = (f32[128,1024]{1,0:T(8,128)S(1)}, f32[128,1024]{1,0:T(8,128)}, u32[]{:S(2)}) copy-start(f32[128,1024]{1,0:T(8,128)} %param.12) | copy-start | bytes 1572868
  58.1 11.1 %all-to-all-start = ((f32[4,128,256]{2,1,0:T(8,128)}), f32[4,128,256]{2,1,0:T(8,128)S(1)}, u32[]{:S(2)}, u32[]{:S(2)}) async-start(f32[4,128,256]{2,1,0:T(8,128)} %get-tuple-element.16), calls=%async_computation | async-start | bytes 1048576 | tf_op jit(solution)/shard_map/all_to_all | solution.py:56
  62.5 8.1 %copy-start.2 = (f32[128,1024]{1,0:T(8,128)S(1)}, f32[128,1024]{1,0:T(8,128)}, u32[]{:S(2)}) copy-start(f32[128,1024]{1,0:T(8,128)} %param.13) | copy-start | bytes 1572868
  70.6 7.6 %copy-start.3 = (f32[128,1024]{1,0:T(8,128)S(1)}, f32[128,1024]{1,0:T(8,128)}, u32[]{:S(2)}) copy-start(f32[128,1024]{1,0:T(8,128)} %param.14) | copy-start | bytes 1572868
  111.2 12.6 %all-to-all-start.1 = ((f32[128,4,256]{2,0,1:T(8,128)}), f32[128,4,256]{2,0,1:T(8,128)S(1)}, u32[]{:S(2)}, u32[]{:S(2)}) async-start(f32[128,4,256]{2,0,1:T(8,128)} %copy.25), calls=%async_computation.1 | async-start | bytes 1048576 | tf_op jit(solution)/shard_map/all_to_all | solution.py:66
  116.6 1.0 copy-start.4
  116.6 1.0 copy-start.5
  116.6 1.0 copy-start.6
  116.6 1.0 copy-start.7
  118.3 5.5 %copy-start = (f32[512,256]{1,0:T(8,128)S(1)}, f32[512,256]{1,0:T(8,128)}, u32[]{:S(2)}) copy-start(f32[512,256]{1,0:T(8,128)} %param.15) | copy-start | bytes 1572868
